TPU v7x, 256 devices: a whole 4x4x8 slice. The times are simulated.
256 devices in a mesh: facet: 16 (over x, y), span: 16 (over z, core).
Axes of the slice: x: 4, y: 4, z: 8, core: 2. Of those that a mesh axis runs over, the one named last changes fastest.
Arguments:
- visibilities: bfloat16 [16, 512, 2, 1024], P('span', 'facet'), may hold values from -6 to 6
- coordinates: bfloat16 [16, 512, 2, 1024], P('span', 'facet'), may hold values from 4 to 124
- phases: float32 [16, 512, 1024], P('span', 'facet'), may hold values from -3.140625 to 3.140625
- sub_index: int32 [16, 512], replicated, may hold values from 0 to 4095, as said below
Outputs:
- dirty: float32 [8192, 8192], P(('facet', 'span'))
Inputs may be any that keep to these rules, and one draw needn't show every extreme that they name: `sub_index`: within one span (one row) all 512 subgrid indices differ. A grid block is the set of subgrids with rows f * 4 to (f + 1) * 4 - 1 and columns j * 4 to (j + 1) * 4 - 1 for f < 16, j < 16; at most 4 indices of one row fall in one grid block, and in every row some grid block holds exactly 4 of them.
All inputs are finite; a program needn't handle non-finite values.
Results may differ from a plain program's by a relative error of at most 0.005.
Values may be sent and summed in bfloat16 or wider, within the bound.
No kernel may reach another device: no remote copies, remote signals or barrier semaphores. Data moves between devices by JAX's collectives and lax.ppermute only.
A program may use at most 64 MiB of HBM per device.

v0:
```python
import jax
import jax.numpy as jnp
from jax import lax
from jax.sharding import PartitionSpec as P

N = 8192
P_SIZE = 128
CAP = 4
spread = 0.75


def kernel_rows(positions, cell_index):
    gap_size = cell_index - positions[..., None]
    return jnp.exp(-(gap_size * gap_size) / (2.0 * spread * spread))


def subgrids_of(vis_items, coord_items):
    cell_index = jnp.arange(P_SIZE, dtype=jnp.float32)
    coord_vals = coord_items.astype(jnp.float32)
    row_kernel = kernel_rows(coord_vals[:, 0, :], cell_index)
    col_kernel = kernel_rows(coord_vals[:, 1, :], cell_index).astype(jnp.bfloat16)
    weighted = (vis_items.astype(jnp.float32)[:, :, :, None] * row_kernel[:, None, :, :]).astype(
        jnp.bfloat16
    )
    result = jnp.einsum("ezkp,ekq->ezpq", weighted, col_kernel, preferred_element_type=jnp.float32)
    return result.astype(jnp.bfloat16)


def group_subgrids(group_inputs):
    return subgrids_of(group_inputs[0], group_inputs[1])


def entries(sub_row, target, band_sub, col_sub, span_count):
    side_count = N // P_SIZE
    sub_rows = sub_row // side_count
    sub_cols = sub_row % side_count
    owning_block = sub_rows // band_sub * span_count + sub_cols // col_sub
    local_slot = sub_rows % band_sub * col_sub + sub_cols % col_sub
    inside = (owning_block == target).astype(jnp.int32)
    rank_of = jnp.cumsum(inside) - 1
    picked = (
        (inside[None, :] == 1) & (rank_of[None, :] == jnp.arange(CAP, dtype=jnp.int32)[:, None])
    ).astype(jnp.int32)
    block_num = jnp.arange(sub_row.shape[0], dtype=jnp.int32)
    block_ids = jnp.sum(picked * block_num[None, :], axis=1)
    slot_ids = jnp.sum(picked * local_slot[None, :], axis=1)
    filled = jnp.sum(picked, axis=1) > 0
    return (block_ids, slot_ids, filled)


def phase_table(row_count, col_count, length):
    row_ids = jnp.arange(row_count, dtype=jnp.int32)[:, None]
    col_ids = jnp.arange(col_count, dtype=jnp.int32)[None, :]
    angles = 2.0 * jnp.pi / length * (row_ids * col_ids % length).astype(jnp.float32)
    return (jnp.cos(angles), jnp.sin(angles))


def inverse_dft(real_part, imag_part):
    length = real_part.shape[-1]
    first_len = 64
    second_len = length // first_len
    leading = real_part.shape[:-1]
    split_real = real_part.reshape(leading + (first_len, second_len))
    split_imag = imag_part.reshape(leading + (first_len, second_len))
    highest = lax.Precision.HIGHEST
    cos_first, sin_first = phase_table(first_len, first_len, first_len)
    step_real = jnp.einsum(
        "av,...vb->...ab", cos_first, split_real, precision=highest
    ) - jnp.einsum("av,...vb->...ab", sin_first, split_imag, precision=highest)
    step_imag = jnp.einsum(
        "av,...vb->...ab", cos_first, split_imag, precision=highest
    ) + jnp.einsum("av,...vb->...ab", sin_first, split_real, precision=highest)
    cos_twist, sin_twist = phase_table(first_len, second_len, length)
    twist_real = step_real * cos_twist - step_imag * sin_twist
    twist_imag = step_real * sin_twist + step_imag * cos_twist
    cos_second, sin_second = phase_table(second_len, second_len, second_len)
    out_real = jnp.einsum(
        "...ab,bc->...ac", twist_real, cos_second, precision=highest
    ) - jnp.einsum("...ab,bc->...ac", twist_imag, sin_second, precision=highest)
    out_imag = jnp.einsum(
        "...ab,bc->...ac", twist_real, sin_second, precision=highest
    ) + jnp.einsum("...ab,bc->...ac", twist_imag, cos_second, precision=highest)
    out_real = jnp.swapaxes(out_real, -1, -2).reshape(leading + (length,))
    out_imag = jnp.swapaxes(out_imag, -1, -2).reshape(leading + (length,))
    return (out_real, out_imag)


def shards(visibilities, coordinates, phases, sub_index):
    facet_count = lax.axis_size("facet")
    span_count = lax.axis_size("span")
    side_count = N // P_SIZE
    band_sub = side_count // facet_count
    col_sub = side_count // span_count
    facet_id = lax.axis_index("facet")
    span_id = lax.axis_index("span")
    vis_count = visibilities.shape[3]
    vis_float = visibilities.astype(jnp.float32)
    cosine = jnp.cos(phases)
    sine = jnp.sin(phases)
    real_part = vis_float[:, :, 0, :]
    imag_part = vis_float[:, :, 1, :]
    rotated = jnp.stack(
        [real_part * cosine - imag_part * sine, real_part * sine + imag_part * cosine], axis=2
    ).astype(jnp.bfloat16)
    own_row = lax.dynamic_index_in_dim(sub_index, span_id, 0, keepdims=False)
    targets = facet_id * span_count + jnp.arange(span_count, dtype=jnp.int32)

    def send_table(target):
        return entries(own_row, target, band_sub, col_sub, span_count)

    send_ids, send_slots, send_filled = jax.vmap(send_table)(targets)
    flat_ids = send_ids.reshape(-1)
    flat_filled = send_filled.reshape(-1)
    entry_count = flat_ids.shape[0]
    blank = jnp.zeros((entry_count, 2, vis_count), jnp.bfloat16)
    pieces = (
        lax.all_gather(rotated, "facet", axis=1, tiled=True),
        lax.all_gather(coordinates, "facet", axis=1, tiled=True),
    )
    rows_here = pieces[0].shape[1]
    inside = flat_filled & (flat_ids >= 0) & (flat_ids < rows_here)
    where_row = jnp.clip(flat_ids, 0, rows_here - 1)
    vis_rows = jnp.take(pieces[0][0], where_row, axis=0)
    coord_rows = jnp.take(pieces[1][0], where_row, axis=0)
    keep_mask = inside[:, None, None]
    chosen_vis = jnp.where(keep_mask, vis_rows, blank)
    chosen_coords = jnp.where(keep_mask, coord_rows, blank)
    grouped_vis = chosen_vis.reshape(span_count, CAP, 2, vis_count)
    grouped_coords = chosen_coords.reshape(span_count, CAP, 2, vis_count)
    made_subs = lax.map(group_subgrids, (grouped_vis, grouped_coords))
    arrived = lax.all_to_all(made_subs, "span", split_axis=0, concat_axis=0, tiled=True)
    my_block = facet_id * span_count + span_id

    def recv_table(source_row):
        return entries(source_row, my_block, band_sub, col_sub, span_count)

    recv_ids, recv_slots, recv_filled = jax.vmap(recv_table)(sub_index)
    slots_here = band_sub * col_sub
    slot_range = jnp.arange(slots_here, dtype=jnp.int32)[:, None]
    onehot = (
        (recv_slots.reshape(-1)[None, :] == slot_range) & recv_filled.reshape(-1)[None, :]
    ).astype(jnp.bfloat16)
    items = arrived.reshape(span_count * CAP, 2 * P_SIZE * P_SIZE)
    summed = jnp.dot(onehot, items, preferred_element_type=jnp.float32)
    block = (
        summed.reshape(band_sub, col_sub, 2, P_SIZE, P_SIZE)
        .transpose(2, 0, 3, 1, 4)
        .reshape(2, band_sub * P_SIZE, col_sub * P_SIZE)
    )
    row_block = lax.all_to_all(block, "span", split_axis=1, concat_axis=2, tiled=True)
    half_real, half_imag = inverse_dft(row_block[0], row_block[1])
    half_done = jnp.stack([half_real, half_imag])
    columns = lax.all_to_all(
        lax.all_to_all(half_done, "facet", split_axis=2, concat_axis=1, tiled=True),
        "span",
        split_axis=2,
        concat_axis=1,
        tiled=True,
    )
    row_count = half_done.shape[1]
    col_count = columns.shape[2]
    ordered = (
        columns.reshape(2, span_count, facet_count, row_count, col_count)
        .transpose(0, 4, 2, 1, 3)
        .reshape(2, col_count, N)
    )
    image_real, image_imag = inverse_dft(ordered[0], ordered[1])
    return image_real * (1.0 / N)


def solution(mesh):
    return jax.shard_map(
        shards,
        mesh=mesh,
        in_specs=(
            P("span", "facet", None, None),
            P("span", "facet", None, None),
            P("span", "facet", None),
            P(),
        ),
        out_specs=P(("facet", "span"), None),
        check_vma=False,
    )
```

profile of v0, /device:TPU:1, one launch (start us, length us, event | category | flops | bytes accessed | tf_op | source)
XLA Modules:
  0.0 588.6 jit_solution(86421095488678001)
XLA Ops:
  12.9 49.8 %all-gather.5.cloned.1.call-done = bf16[1,512,2,1024]{3,2,0,1:T(2,128)(2,1)} async-done(((bf16[1,32,2,1024]{3,2,0,1:T(2,128)(2,1)}), bf16[1,512,2,1024]{3,2,0,1:T(2,128)(2,1)}) %all-gather.5.cloned.1.call-update) | async-done | bytes 2097168 | tf_op jit(solution)/shard_map/all_gather | solution.py:118
  62.7 2.7 gather_fusion.1
  65.4 49.1 %all-gather.3.cloned.1.call-done = bf16[1,512,2,1024]{3,2,0,1:T(2,128)(2,1)} async-done(((bf16[1,32,2,1024]{3,2,0,1:T(2,128)(2,1)}), bf16[1,512,2,1024]{3,2,0,1:T(2,128)(2,1)}) %all-gather.3.cloned.1.call-update) | async-done | bytes 2097168 | tf_op jit(solution)/shard_map/all_gather | solution.py:117
  114.6 2.7 gather_fusion
  117.9 90.2 %while.10 = (s32[]{:T(128)}, bf16[16,4,2,128,128]{4,3,2,1,0:T(8,128)(2,1)}, bf16[16,4,2,1024]{3,2,1,0:T(2,128)(2,1)S(1)}, bf16[16,4,2,1024]{3,2,1,0:T(2,128)(2,1)S(1)}, s32[]{:T(128)}) while((s32[]{:T(128)}, bf16[16,4,2,128,128]{4,3,2,1,0:T(8,128)(2,1)}, bf16[16,4,2,1024]{3,2,1,0:T(2,128)(2,1)S(1)}, bf16[16,4,2,1024]{3,2,1,0:T(2,128)(2,1)S(1)}, ...), condition=%wide.region_9.11_spmd, body=%wide.region_8.10_spmd.sunk | while | flops 275398656 | bytes 8912977 | solution.py:130
  120.5 3.1 fusion.190
  126.2 3.1 fusion.190
  131.8 3.1 fusion.190
  137.4 3.1 fusion.190
  143.1 3.1 fusion.190
  148.7 3.1 fusion.190
  154.3 3.1 fusion.190
  160.0 3.1 fusion.190
  165.6 3.1 fusion.190
  171.2 3.1 fusion.190
  176.9 3.1 fusion.190
  182.5 3.1 fusion.190
  188.1 3.1 fusion.190
  193.8 3.1 fusion.190
  199.4 3.1 fusion.190
  205.0 3.1 fusion.190
  208.1 8.5 %all-to-all-start = ((bf16[16,4,2,128,128]{4,3,2,1,0:T(8,128)(2,1)}), bf16[16,4,2,128,128]{4,3,2,1,0:T(8,128)(2,1)}, u32[]{:S(2)}, u32[]{:S(2)}) async-start(bf16[16,4,2,128,128]{4,3,2,1,0:T(8,128)(2,1)} %get-tuple-element.28), calls=%async_computation | async-start | bytes 8388608 | tf_op jit(solution)/shard_map/all_to_all | solution.py:131
  218.9 91.3 %all-to-all-done = bf16[16,4,2,128,128]{4,3,2,1,0:T(8,128)(2,1)} async-done(((bf16[16,4,2,128,128]{4,3,2,1,0:T(8,128)(2,1)}), bf16[16,4,2,128,128]{4,3,2,1,0:T(8,128)(2,1)}, u32[]{:S(2)}, u32[]{:S(2)}) %all-to-all-start) | async-done | bytes 4194336 | tf_op jit(solution)/shard_map/all_to_all | solution.py:131
  310.2 7.3 %reshape.280 = bf16[64,32768]{1,0:T(8,128)(2,1)} reshape(bf16[16,4,2,128,128]{4,3,2,1,0:T(8,128)(2,1)} %all-to-all-done) | data formatting | bytes 8388608 | tf_op jit(solution)/shard_map/reshape | solution.py:143
  317.5 3.3 copy.148
  320.9 2.6 fusion.15
  323.8 2.6 reshape.314
  326.5 5.8 all-to-all-start.1
  332.4 48.7 %all-to-all-done.1 = f32[2,512,512]{2,0,1:T(2,128)S(1)} async-done(((f32[2,512,512]{2,0,1:T(2,128)}), f32[2,512,512]{2,0,1:T(2,128)S(1)}, u32[]{:S(2)}, u32[]{:S(2)}) %all-to-all-start.1) | async-done | bytes 2097184 | tf_op jit(solution)/shard_map/all_to_all | solution.py:150
  382.5 2.1 fusion.76
  390.1 2.2 fusion.38
  393.6 2.0 copy.129
  395.5 2.3 stack_reshape.7
  397.9 3.4 fusion.23
  406.1 7.9 %copy.130 = f32[2,32,8192]{1,0,2:T(2,128)} copy(f32[2,32,8192]{2,1,0:T(8,128)S(1)} %pad_maximum_fusion) | data formatting | bytes 4194304 | tf_op jit(solution)/shard_map/stack | solution.py:152
  414.0 10.3 %reshape.317 = f32[16,1,32768]{2,1,0:T(1,128)S(1)} reshape(f32[8192,2,32]{2,1,0:T(2,128)} %bitcast.179) | data formatting | bytes 4194304
  424.3 31.8 %all_to_all.53 = f32[16,1,32768]{2,1,0:T(1,128)} all-to-all(f32[16,1,32768]{2,1,0:T(1,128)S(1)} %reshape.317), channel_id=1, replica_groups=mesh['facet'=16,'span'=16] {'facet'}, dimensions={0} | all-to-all | bytes 4194304 | tf_op jit(solution)/shard_map/all_to_all | solution.py:154
  456.6 7.3 %reduce.4 = f32[16,32768]{1,0:T(8,128)S(1)} reduce(f32[16,1,32768]{2,1,0:T(1,128)} %all_to_all.53, f32[]{:T(128)} %broadcast.473), dimensions={1}, to_apply=%all_to_all.42.reduce_sub_computation | reduce | bytes 4194308 | tf_op jit(solution)/shard_map/all_to_all | solution.py:154
  463.9 9.0 %reshape.318 = f32[8192,2,32]{2,1,0:T(2,128)} reshape(f32[16,32768]{1,0:T(8,128)S(1)} %reduce.4) | data formatting | bytes 4194304
  472.9 10.2 %copy.142 = f32[2,32,16,512]{3,1,2,0:T(8,128)S(1)} copy(f32[2,32,16,512]{1,0,3,2:T(2,128)} %bitcast.180) | data formatting | bytes 4194304 | tf_op jit(solution)/shard_map/all_to_all | solution.py:154
  483.1 2.5 copy.133
  485.6 58.1 %all_to_all.54 = f32[2,512,512]{1,0,2:T(2,128)S(1)} all-to-all(f32[2,512,512]{1,0,2:T(2,128)} %copy.133), channel_id=1, replica_groups=mesh['facet'=16,'span'=16] {'span'}, dimensions={2} | all-to-all | bytes 4194304 | tf_op jit(solution)/shard_map/all_to_all | solution.py:153
  544.0 4.4 reshape.282
  548.5 6.1 %fusion.174 = (f32[1,32,16,16,32]{4,2,1,3,0:T(8,128)S(1)}, f32[1,32,16,16,32]{4,2,1,3,0:T(8,128)}) fusion(f32[2,32,16,16,32]{4,2,1,3,0:T(8,128)} %bitcast.181), kind=kLoop, calls=%fused_computation.251 | loop fusion | bytes 4194304 | tf_op jit(solution)/shard_map/slice | solution.py:167
  554.6 4.4 copy.135
  558.9 3.3 reshape_squeeze.14
  563.4 6.5 %copy.136 = f32[1,32,16,16,32]{4,3,2,1,0:T(8,128)} copy(f32[1,32,16,16,32]{4,2,1,3,0:T(8,128)} %get-tuple-element.70) | data formatting | bytes 2097152 | tf_op jit(solution)/shard_map/slice | solution.py:167
  569.9 3.4 reshape_squeeze.15
  (171 shorter events, 73.1 us)
Async XLA Ops:
  6.5 4.0 copy-start.1
  6.5 56.2 %all-gather.5.cloned.1.call-start = ((), (), s32[]{:S(2)}) async-start(), calls=%async_computation.5 | async-start | bytes 2228224 | tf_op jit(solution)/shard_map/all_gather | solution.py:118
  7.3 107.3 %all-gather.3.cloned.1.call-start = ((), (), s32[]{:S(2)}) async-start(), calls=%async_computation.4 | async-start | bytes 2228224 | tf_op jit(solution)/shard_map/all_gather | solution.py:117
  208.1 102.1 %all-to-all-start = ((bf16[16,4,2,128,128]{4,3,2,1,0:T(8,128)(2,1)}), bf16[16,4,2,128,128]{4,3,2,1,0:T(8,128)(2,1)}, u32[]{:S(2)}, u32[]{:S(2)}) async-start(bf16[16,4,2,128,128]{4,3,2,1,0:T(8,128)(2,1)} %get-tuple-element.28), calls=%async_computation | async-start | bytes 8388608 | tf_op jit(solution)/shard_map/all_to_all | solution.py:131
  326.5 54.6 %all-to-all-start.1 = ((f32[2,512,512]{2,0,1:T(2,128)}), f32[2,512,512]{2,0,1:T(2,128)S(1)}, u32[]{:S(2)}, u32[]{:S(2)}) async-start(f32[2,512,512]{2,0,1:T(2,128)} %reshape.314), calls=%async_computation.1 | async-start | bytes 4194304 | tf_op jit(solution)/shard_map/all_to_all | solution.py:150
  385.3 1.2 copy-start
Sparse Core Ops, SparseCore 0:
  9.8 52.8 all-gather.4
  65.2 49.3 all-gather.2
where the time goes:
time: 598 us; the launch traced here: 589 us
  waiting for transfers between devices  240 us (40%)
  local copies, waits for them, and re-layouts  133 us (22%)
  blocking collectives  89.9 us (15%)
  matrix products  72.7 us (12%)
  other arithmetic  24.1 us (4%)
  starting transfers between devices  14.4 us (2%)
  between operations  14 us (2%)
    all_to_all x1, waiting for transfers between devices, shards(): lax.all_to_all(made_subs, 'span', split_axis=0, concat_axis=0, tiled=True)  91.3 us
    all_to_all x1, blocking collectives, shards(): lax.all_to_all(lax.all_to_all(half_done, 'facet', split_axis=2, concat_ax...  58.1 us
    all_gather x1, waiting for transfers between devices, shards(): lax.all_gather(coordinates, 'facet', axis=1, tiled=True)  49.8 us
    dot_general x16, matrix products, subgrids_of(): jnp.einsum('ezkp,ekq->ezpq', weighted, col_kernel, preferred_element_type...  49.2 us
    all_gather x1, waiting for transfers between devices, shards(): lax.all_gather(rotated, 'facet', axis=1, tiled=True)  49.1 us
    all_to_all x1, waiting for transfers between devices, shards(): lax.all_to_all(block, 'span', split_axis=1, concat_axis=2, tiled=True)  48.7 us
    all_to_all x1, blocking collectives, shards(): lax.all_to_all(half_done, 'facet', split_axis=2, concat_axis=1, tiled=True)  31.8 us
    exp x16, local copies, waits for them, and re-layouts, kernel_rows(): return jnp.exp(-(gap_size * gap_size) / (2.0 * spread * spread))  29.8 us
  transfers between devices with their start and end apart: 4, of which 4 were waited for; matrix products, arithmetic and copies ran while one was open for 2% of the time, Pallas kernels for 0%

commit v1 on v0

--- a/solution.py
+++ b/solution.py
@@ -151,7 +151,12 @@
     half_real, half_imag = inverse_dft(row_block[0], row_block[1])
     half_done = jnp.stack([half_real, half_imag])
     columns = lax.all_to_all(
-        lax.all_to_all(half_done, "facet", split_axis=2, concat_axis=1, tiled=True),
+        jnp.concatenate(
+            lax.all_to_all(
+                jnp.stack(jnp.split(half_done, lax.axis_size("facet"), axis=2)), "facet", 0, 0
+            ),
+            axis=1,
+        ),
         "span",
         split_axis=2,
         concat_axis=1,

time: 598 us -> 553 us (0.925)
  local copies, waits for them, and re-layouts: 133 us -> 97.3 us
  other arithmetic: 24.1 us -> 15.5 us
    unnamed x7 -> x21, local copies, waits for them, and re-layouts: 22.7 us -> 4.86 us
    all_to_all x4 -> x1, local copies, waits for them, and re-layouts: 13.5 us -> 0.41 us  [shards(): lax.all_to_all(jnp.concatenate(lax.all_to_all(jnp.stack(jnp.split(half_do...]
    another operation x3, local copies, waits for them, and re-layouts: 11.8 us -> 3.99 us  [shards(): half_done = jnp.stack([half_real, half_imag])]
    all_to_all x1 -> x0, other arithmetic: 7.29 us -> none  [shards(): lax.all_to_all(half_done, 'facet', split_axis=2, concat_axis=1, tiled=True)]
where the time goes in v1:
time: 553 us; the launch traced here: 544 us
  waiting for transfers between devices  240 us (43%)
  local copies, waits for them, and re-layouts  97.3 us (18%)
  blocking collectives  89.3 us (16%)
  matrix products  72.7 us (13%)
  other arithmetic  15.5 us (3%)
  starting transfers between devices  14.7 us (3%)
  between operations  14.1 us (3%)
    all_to_all x1, waiting for transfers between devices, shards(): lax.all_to_all(made_subs, 'span', split_axis=0, concat_axis=0, tiled=True)  91.3 us
    all_to_all x1, blocking collectives, shards(): lax.all_to_all(jnp.concatenate(lax.all_to_all(jnp.stack(jnp.split(half_do...  57.7 us
    all_gather x1, waiting for transfers between devices, shards(): lax.all_gather(coordinates, 'facet', axis=1, tiled=True)  49.8 us
    dot_general x16, matrix products, subgrids_of(): jnp.einsum('ezkp,ekq->ezpq', weighted, col_kernel, preferred_element_type...  49.2 us
    all_gather x1, waiting for transfers between devices, shards(): lax.all_gather(rotated, 'facet', axis=1, tiled=True)  49.1 us
    all_to_all x1, waiting for transfers between devices, shards(): lax.all_to_all(block, 'span', split_axis=1, concat_axis=2, tiled=True)  48.7 us
    all_to_all x1, blocking collectives, shards(): lax.all_to_all(jnp.stack(jnp.split(half_done, lax.axis_size('facet'), axi...  31.7 us
    exp x16, local copies, waits for them, and re-layouts, kernel_rows(): return jnp.exp(-(gap_size * gap_size) / (2.0 * spread * spread))  29.8 us
  transfers between devices with their start and end apart: 4, of which 4 were waited for; matrix products, arithmetic and copies ran while one was open for 2% of the time, Pallas kernels for 0%

profile of v1, /device:TPU:1, one launch (start us, length us, event | category | flops | bytes accessed | tf_op | source)
XLA Modules:
  0.0 543.8 jit_solution(13539272184350999357)
XLA Ops:
  12.9 49.8 %all-gather.5.cloned.1.call-done = bf16[1,512,2,1024]{3,2,0,1:T(2,128)(2,1)} async-done(((bf16[1,32,2,1024]{3,2,0,1:T(2,128)(2,1)}), bf16[1,512,2,1024]{3,2,0,1:T(2,128)(2,1)}) %all-gather.5.cloned.1.call-update) | async-done | bytes 2097168 | tf_op jit(solution)/shard_map/all_gather | solution.py:118
  62.7 2.7 gather_fusion.1
  65.4 49.1 %all-gather.3.cloned.1.call-done = bf16[1,512,2,1024]{3,2,0,1:T(2,128)(2,1)} async-done(((bf16[1,32,2,1024]{3,2,0,1:T(2,128)(2,1)}), bf16[1,512,2,1024]{3,2,0,1:T(2,128)(2,1)}) %all-gather.3.cloned.1.call-update) | async-done | bytes 2097168 | tf_op jit(solution)/shard_map/all_gather | solution.py:117
  114.6 2.7 gather_fusion
  117.9 90.1 %while.10 = (s32[]{:T(128)}, bf16[16,4,2,128,128]{4,3,2,1,0:T(8,128)(2,1)}, bf16[16,4,2,1024]{3,2,1,0:T(2,128)(2,1)S(1)}, bf16[16,4,2,1024]{3,2,1,0:T(2,128)(2,1)S(1)}, s32[]{:T(128)}) while((s32[]{:T(128)}, bf16[16,4,2,128,128]{4,3,2,1,0:T(8,128)(2,1)}, bf16[16,4,2,1024]{3,2,1,0:T(2,128)(2,1)S(1)}, bf16[16,4,2,1024]{3,2,1,0:T(2,128)(2,1)S(1)}, ...), condition=%wide.region_9.11_spmd, body=%wide.region_8.10_spmd.sunk | while | flops 275398656 | bytes 8912977 | solution.py:130
  118.7 1.9 copy.137
  120.5 3.1 fusion.206
  126.1 3.1 fusion.206
  129.9 1.9 copy.137
  131.8 3.1 fusion.206
  137.4 3.1 fusion.206
  141.2 1.9 copy.137
  143.0 3.1 fusion.206
  148.7 3.1 fusion.206
  152.5 1.9 copy.137
  154.3 3.1 fusion.206
  158.1 1.9 copy.137
  160.0 3.1 fusion.206
  165.6 3.1 fusion.206
  171.2 3.1 fusion.206
  176.9 3.1 fusion.206
  182.5 3.1 fusion.206
  188.1 3.1 fusion.206
  193.8 3.1 fusion.206
  199.4 3.1 fusion.206
  205.0 3.1 fusion.206
  208.1 8.5 %all-to-all-start = ((bf16[16,4,2,128,128]{4,3,2,1,0:T(8,128)(2,1)}), bf16[16,4,2,128,128]{4,3,2,1,0:T(8,128)(2,1)}, u32[]{:S(2)}, u32[]{:S(2)}) async-start(bf16[16,4,2,128,128]{4,3,2,1,0:T(8,128)(2,1)} %get-tuple-element.28), calls=%async_computation | async-start | bytes 8388608 | tf_op jit(solution)/shard_map/all_to_all | solution.py:131
  218.9 91.3 %all-to-all-done = bf16[16,4,2,128,128]{4,3,2,1,0:T(8,128)(2,1)} async-done(((bf16[16,4,2,128,128]{4,3,2,1,0:T(8,128)(2,1)}), bf16[16,4,2,128,128]{4,3,2,1,0:T(8,128)(2,1)}, u32[]{:S(2)}, u32[]{:S(2)}) %all-to-all-start) | async-done | bytes 4194336 | tf_op jit(solution)/shard_map/all_to_all | solution.py:131
  310.2 7.3 %reshape.286 = bf16[64,32768]{1,0:T(8,128)(2,1)} reshape(bf16[16,4,2,128,128]{4,3,2,1,0:T(8,128)(2,1)} %all-to-all-done) | data formatting | bytes 8388608 | tf_op jit(solution)/shard_map/reshape | solution.py:143
  317.5 3.3 copy.120
  320.9 2.6 fusion.15
  323.8 2.6 reshape.322
  326.5 6.1 %all-to-all-start.1 = ((f32[2,512,512]{2,0,1:T(2,128)}), f32[2,512,512]{2,0,1:T(2,128)S(1)}, u32[]{:S(2)}, u32[]{:S(2)}) async-start(f32[2,512,512]{2,0,1:T(2,128)} %reshape.322), calls=%async_computation.1 | async-start | bytes 4194304 | tf_op jit(solution)/shard_map/all_to_all | solution.py:150
  332.7 48.7 %all-to-all-done.1 = f32[2,512,512]{2,0,1:T(2,128)S(1)} async-done(((f32[2,512,512]{2,0,1:T(2,128)}), f32[2,512,512]{2,0,1:T(2,128)S(1)}, u32[]{:S(2)}, u32[]{:S(2)}) %all-to-all-start.1) | async-done | bytes 2097184 | tf_op jit(solution)/shard_map/all_to_all | solution.py:150
  382.8 2.1 fusion.92
  390.4 2.2 fusion.38
  393.9 2.0 copy.105
  395.8 2.3 stack_reshape.7
  398.1 3.4 fusion.23
  406.7 31.7 %all_to_all.40 = f32[16,2,32,512]{3,2,1,0:T(8,128)S(1)} all-to-all(f32[16,2,32,512]{3,2,1,0:T(8,128)S(1)} %fusion.39), channel_id=1, replica_groups=mesh['facet'=16,'span'=16] {'facet'}, dimensions={0} | all-to-all | bytes 4194304 | tf_op jit(solution)/shard_map/all_to_all | solution.py:155
  438.6 2.5 copy.107
  441.1 57.7 %all_to_all.41 = f32[2,512,512]{1,0,2:T(2,128)S(1)} all-to-all(f32[2,512,512]{1,0,2:T(2,128)} %copy.107), channel_id=1, replica_groups=mesh['facet'=16,'span'=16] {'span'}, dimensions={2} | all-to-all | bytes 4194304 | tf_op jit(solution)/shard_map/all_to_all | solution.py:153
  499.2 4.4 reshape.290
  503.6 6.1 %fusion.190 = (f32[1,32,16,16,32]{4,2,1,3,0:T(8,128)S(1)}, f32[1,32,16,16,32]{4,2,1,3,0:T(8,128)}) fusion(f32[2,32,16,16,32]{4,2,1,3,0:T(8,128)} %bitcast.238), kind=kLoop, calls=%fused_computation.284 | loop fusion | bytes 4194304 | tf_op jit(solution)/shard_map/slice | solution.py:172
  509.7 4.4 copy.109
  514.0 3.3 reshape_squeeze.14
  518.5 6.5 %copy.110 = f32[1,32,16,16,32]{4,3,2,1,0:T(8,128)} copy(f32[1,32,16,16,32]{4,2,1,3,0:T(8,128)} %get-tuple-element.66) | data formatting | bytes 2097152 | tf_op jit(solution)/shard_map/slice | solution.py:172
  525.0 3.5 reshape_squeeze.15
  (183 shorter events, 63.8 us)
Async XLA Ops:
  6.5 4.0 copy-start.1
  6.5 56.2 %all-gather.5.cloned.1.call-start = ((), (), s32[]{:S(2)}) async-start(), calls=%async_computation.5 | async-start | bytes 2228224 | tf_op jit(solution)/shard_map/all_gather | solution.py:118
  7.3 107.3 %all-gather.3.cloned.1.call-start = ((), (), s32[]{:S(2)}) async-start(), calls=%async_computation.4 | async-start | bytes 2228224 | tf_op jit(solution)/shard_map/all_gather | solution.py:117
  208.1 102.1 %all-to-all-start = ((bf16[16,4,2,128,128]{4,3,2,1,0:T(8,128)(2,1)}), bf16[16,4,2,128,128]{4,3,2,1,0:T(8,128)(2,1)}, u32[]{:S(2)}, u32[]{:S(2)}) async-start(bf16[16,4,2,128,128]{4,3,2,1,0:T(8,128)(2,1)} %get-tuple-element.28), calls=%async_computation | async-start | bytes 8388608 | tf_op jit(solution)/shard_map/all_to_all | solution.py:131
  326.5 54.9 %all-to-all-start.1 = ((f32[2,512,512]{2,0,1:T(2,128)}), f32[2,512,512]{2,0,1:T(2,128)S(1)}, u32[]{:S(2)}, u32[]{:S(2)}) async-start(f32[2,512,512]{2,0,1:T(2,128)} %reshape.322), calls=%async_computation.1 | async-start | bytes 4194304 | tf_op jit(solution)/shard_map/all_to_all | solution.py:150
  385.6 1.2 copy-start
Sparse Core Ops, SparseCore 0:
  9.8 52.8 all-gather.4
  65.2 49.3 all-gather.2
